TPU v7x, 32 devices: a whole 2x2x4 slice. The times are simulated.
32 devices in a mesh: mem: 8 (over y, x, core), st: 4 (over z).
Axes of the slice: x: 2, y: 2, z: 4, core: 2. Of those that a mesh axis runs over, the one named last changes fastest.
Arguments:
- ensemble: float32 [8192, 256], P('st', 'mem'), may hold values from -8 to 8
- obs_values: float32 [4, 8, 128], replicated, may hold values from -8 to 8
- obs_sigma: float32 [4, 8, 128], replicated, may hold values from 0.25 to 0.5
- obs_operator: float32 [4, 8, 2, 128, 128], replicated, may hold values from -0.375 to 0.375
- block_cols: int32 [4, 8, 2], replicated, may hold values from 0 to 63
- batch_order: int32 [4], replicated, may hold values from 0 to 3, each once
Outputs:
- analysis: float32 [8192, 256], P('st', 'mem')
- log_weights: float32 [256], P('mem')
- ess: float32 [], replicated
Inputs may be any that keep to these rules, and one draw needn't show every extreme that they name: `block_cols`: block indices of the whole state. `batch_order`: each batch exactly once.
All inputs are finite; a program needn't handle non-finite values.
Results may differ from a plain program's by a relative error of at most 0.0003.
Values sent between devices are 32-bit elements; how exact they have to be, the bound alone decides.
A program may use at most 64 MiB of HBM per device.

v0:
```python
import math
import jax
import jax.numpy as jnp
from jax import lax
from jax.sharding import PartitionSpec as P

precise = lax.Precision.HIGHEST


def solve_blocks(moment, target):
    factor = jnp.linalg.cholesky(moment)
    return jax.vmap(lambda lower, right: jax.scipy.linalg.cho_solve((lower, True), right))(
        factor, target
    )


def shards(ensemble, obs_values, obs_sigma, obs_operator, block_cols, batch_order):
    block_size = obs_operator.shape[-1]
    row_count, mem_dev = ensemble.shape
    nblocks = row_count // block_size
    members = mem_dev * lax.axis_size("mem")
    batches, obs_blocks, col_count = block_cols.shape
    temper = 1.0 / math.sqrt(batches * obs_blocks * block_size)
    offset = lax.axis_index("st") * nblocks
    states = ensemble.reshape(nblocks, block_size, mem_dev)
    eye = jnp.eye(block_size, dtype=jnp.float32)
    slots = jnp.arange(nblocks, dtype=jnp.int32)
    loglik = jnp.zeros((mem_dev,), jnp.float32)
    for batch_step in range(batches):
        chosen = batch_order[batch_step]
        operator_now = lax.dynamic_index_in_dim(obs_operator, chosen, 0, keepdims=False)
        columns = lax.dynamic_index_in_dim(block_cols, chosen, 0, keepdims=False)
        values_now = lax.dynamic_index_in_dim(obs_values, chosen, 0, keepdims=False)
        sigma_now = lax.dynamic_index_in_dim(obs_sigma, chosen, 0, keepdims=False)
        local_ids = columns.reshape(-1) - offset
        selector = (local_ids[:, None] == slots[None, :]).astype(jnp.float32)
        picked = jnp.einsum("ps,sim->pim", selector, states, precision=precise)
        picked = picked.reshape(obs_blocks, col_count, block_size, mem_dev)
        partial_value = jnp.einsum("bkij,bkjm->bim", operator_now, picked, precision=precise)
        image = lax.psum(partial_value, "st")
        misfit = (values_now[:, :, None] - image) / sigma_now[:, :, None]
        loglik = loglik - 0.5 * temper * jnp.sum(misfit * misfit, axis=(0, 1))
        center = lax.psum(jnp.sum(image, axis=2), "mem") / members
        anomaly = image - center[:, :, None]
        moment_sum, cross_sum = lax.psum(
            (
                jnp.einsum("bim,bjm->bij", anomaly, anomaly, precision=precise),
                jnp.einsum("bkim,bjm->bkij", picked, anomaly, precision=precise),
            ),
            "mem",
        )
        moment = moment_sum / (members - 1) + eye * (sigma_now * sigma_now)[:, :, None]
        cross = cross_sum / (members - 1)
        target = (values_now - center)[:, :, None] - 0.5 * anomaly
        weights = solve_blocks(moment, target)
        change = jnp.einsum("bkij,bjm->bkim", cross, weights, precision=precise)
        change = change.reshape(obs_blocks * col_count, block_size, mem_dev)
        states = states + jnp.einsum("ps,pim->sim", selector, change, precision=precise)
    largest_local = jnp.max(loglik)
    largest = lax.pmax(largest_local, "mem")
    scaled = jnp.exp(loglik - largest)
    summed, squares = lax.psum((jnp.sum(scaled), jnp.sum(scaled * scaled)), "mem")
    log_weights = loglik - largest - jnp.log(summed)
    ess = summed * summed / squares
    return (states.reshape(row_count, mem_dev), log_weights, ess)


def solution(mesh):
    placed = (P("st", "mem"), P(), P(), P(), P(), P())
    return jax.shard_map(
        shards,
        mesh=mesh,
        in_specs=placed,
        out_specs=(P("st", "mem"), P("mem"), P()),
        check_vma=False,
    )
```

profile of v0, /device:TPU:0, one launch (start us, length us, event | category | flops | bytes accessed | tf_op | source)
XLA Modules:
  0.0 1220.0 jit_solution(10032874839914542183)
XLA Ops:
  7.2 1.5 fusion.151
  18.7 3.1 convolution_bitcast_fusion.7
  23.3 35.7 %all-reduce.14.cloned.1.call-done = f32[8,128,32]{1,2,0:T(8,128)} async-done(((f32[8,128,32]{1,2,0:T(8,128)}), f32[8,128,32]{1,2,0:T(8,128)}) %all-reduce.14.cloned.1.call-update) | async-done | bytes 131088 | tf_op jit(solution)/shard_map/psum | solution.py:40
  60.1 11.8 psum.127
  71.9 3.9 fusion.50
  75.8 2.9 fusion.77
  79.3 57.4 %all-reduce.28.cloned.1.call-done = (f32[8,128,128]{1,2,0:T(8,128)}, f32[8,2,128,128]{3,2,1,0:T(8,128)}) async-done(((f32[8,128,128]{1,2,0:T(8,128)}, f32[8,2,128,128]{3,2,1,0:T(8,128)}), (f32[8,128,128]{1,2,0:T(8,128)}, f32[8,2,128,128]{3,2,1,0:T(8,128)})) %all-reduce.28.cloned.1.call-update) | async-done | bytes 1572880 | tf_op jit(solution)/shard_map/psum | solution.py:45
  136.7 1.2 multiply_add_fusion.3
  138.1 1.1 fusion.31
  139.2 93.8 %custom-call.14 = f32[8,128,128]{2,1,0:T(8,128)S(1)} custom-call(f32[8,128,128]{2,1,0:T(8,128)S(1)} %fusion.31), custom_call_target="Cholesky" | custom-call | tf_op jit(solution)/shard_map/jit(cholesky)/cholesky | solution.py:11
  233.3 78.6 %custom-call.15 = f32[8,1,128,128]{2,3,1,0:T(8,128)S(1)} custom-call(f32[8,1,128,128]{3,2,1,0:T(8,128)S(1)} %select_bitcast_fusion.3), custom_call_target="InvertDiagBlocksLowerTriangular" | custom-call | tf_op jit(solution)/shard_map/vmap(jit(_cho_solve))/triangular_solve | solution.py:12
  313.4 1.2 fusion.13
  315.3 3.1 convolution_bitcast_fusion.6
  318.5 33.9 %all-reduce.16.cloned.1.call-done = f32[8,128,32]{1,2,0:T(8,128)} async-done(((f32[8,128,32]{1,2,0:T(8,128)}), f32[8,128,32]{1,2,0:T(8,128)}) %all-reduce.16.cloned.1.call-update) | async-done | bytes 131088 | tf_op jit(solution)/shard_map/psum | solution.py:40
  353.4 12.0 psum.131
  365.4 3.9 fusion.47
  369.3 2.9 fusion.73
  372.4 57.8 %all-reduce.26.cloned.1.call-done = (f32[8,128,128]{1,2,0:T(8,128)}, f32[8,2,128,128]{3,2,1,0:T(8,128)}) async-done(((f32[8,128,128]{1,2,0:T(8,128)}, f32[8,2,128,128]{3,2,1,0:T(8,128)}), (f32[8,128,128]{1,2,0:T(8,128)}, f32[8,2,128,128]{3,2,1,0:T(8,128)})) %all-reduce.26.cloned.1.call-update) | async-done | bytes 1572880 | tf_op jit(solution)/shard_map/psum | solution.py:45
  430.2 1.2 multiply_add_fusion.2
  431.6 1.1 fusion.27
  432.8 93.8 %custom-call.16 = f32[8,128,128]{2,1,0:T(8,128)S(1)} custom-call(f32[8,128,128]{2,1,0:T(8,128)S(1)} %fusion.27), custom_call_target="Cholesky" | custom-call | tf_op jit(solution)/shard_map/jit(cholesky)/cholesky | solution.py:11
  526.9 78.6 %custom-call.17 = f32[8,1,128,128]{2,3,1,0:T(8,128)S(1)} custom-call(f32[8,1,128,128]{3,2,1,0:T(8,128)S(1)} %select_bitcast_fusion.2), custom_call_target="InvertDiagBlocksLowerTriangular" | custom-call | tf_op jit(solution)/shard_map/vmap(jit(_cho_solve))/triangular_solve | solution.py:12
  607.0 1.2 fusion.10
  608.9 3.1 convolution_bitcast_fusion.5
  612.0 33.9 %all-reduce.18.cloned.1.call-done = f32[8,128,32]{1,2,0:T(8,128)} async-done(((f32[8,128,32]{1,2,0:T(8,128)}), f32[8,128,32]{1,2,0:T(8,128)}) %all-reduce.18.cloned.1.call-update) | async-done | bytes 131088 | tf_op jit(solution)/shard_map/psum | solution.py:40
  647.0 12.2 %psum.135 = f32[8,128]{1,0:T(8,128)S(1)} all-reduce(f32[8,128]{1,0:T(8,128)S(1)} %get-tuple-element.10), channel_id=1, replica_groups=mesh['mem'=8,'st'=4] {'mem'}, use_global_device_ids=true, to_apply=%region_14.17 | all-reduce | flops 1024 | bytes 8192 | tf_op jit(solution)/shard_map/psum | solution.py:43
  659.2 3.9 fusion.44
  663.1 2.9 fusion.69
  666.2 57.8 %all-reduce.24.cloned.1.call-done = (f32[8,128,128]{1,2,0:T(8,128)}, f32[8,2,128,128]{3,2,1,0:T(8,128)}) async-done(((f32[8,128,128]{1,2,0:T(8,128)}, f32[8,2,128,128]{3,2,1,0:T(8,128)}), (f32[8,128,128]{1,2,0:T(8,128)}, f32[8,2,128,128]{3,2,1,0:T(8,128)})) %all-reduce.24.cloned.1.call-update) | async-done | bytes 1572880 | tf_op jit(solution)/shard_map/psum | solution.py:45
  724.0 1.2 multiply_add_fusion.1
  725.4 1.1 fusion.23
  726.5 93.8 %custom-call.18 = f32[8,128,128]{2,1,0:T(8,128)S(1)} custom-call(f32[8,128,128]{2,1,0:T(8,128)S(1)} %fusion.23), custom_call_target="Cholesky" | custom-call | tf_op jit(solution)/shard_map/jit(cholesky)/cholesky | solution.py:11
  820.6 78.6 %custom-call.19 = f32[8,1,128,128]{2,3,1,0:T(8,128)S(1)} custom-call(f32[8,1,128,128]{3,2,1,0:T(8,128)S(1)} %select_bitcast_fusion.1), custom_call_target="InvertDiagBlocksLowerTriangular" | custom-call | tf_op jit(solution)/shard_map/vmap(jit(_cho_solve))/triangular_solve | solution.py:12
  900.7 1.2 fusion.7
  902.6 3.1 convolution_bitcast_fusion.4
  905.8 33.9 %all-reduce.20.cloned.1.call-done = f32[8,128,32]{1,2,0:T(8,128)} async-done(((f32[8,128,32]{1,2,0:T(8,128)}), f32[8,128,32]{1,2,0:T(8,128)}) %all-reduce.20.cloned.1.call-update) | async-done | bytes 131088 | tf_op jit(solution)/shard_map/psum | solution.py:40
  941.3 12.4 %pmax.7 = f32[]{:T(128)} all-reduce(f32[]{:T(128)} %get-tuple-element.28), channel_id=1, replica_groups=mesh['mem'=8,'st'=4] {'mem'}, use_global_device_ids=true, to_apply=%region_27.30 | all-reduce | flops 1 | bytes 8 | tf_op jit(solution)/shard_map/pmax | solution.py:60
  953.7 1.3 multiply_reduce_fusion.4
  955.0 12.8 %all-reduce = (f32[8,128]{1,0:T(8,128)S(1)}, f32[]{:T(128)}, f32[]{:T(128)}) all-reduce(f32[8,128]{1,0:T(8,128)S(1)} %get-tuple-element.12, f32[]{:T(128)} %get-tuple-element.14, f32[]{:T(128)} %get-tuple-element.13), channel_id=1, replica_groups=mesh['mem'=8,'st'=4] {'mem'}, use_global_device_ids=true, to_apply=%region_19.22 | all-reduce | flops 1026 | bytes 8208 | tf_op jit(solution)/shard_map/psum | solution.py:43
  967.8 3.9 fusion.41
  971.7 2.9 fusion.65
  977.3 1.2 broadcast_subtract_fusion
  978.4 54.3 %all-reduce.22.cloned.1.call-done = (f32[8,128,128]{1,2,0:T(8,128)}, f32[8,2,128,128]{3,2,1,0:T(8,128)}) async-done(((f32[8,128,128]{1,2,0:T(8,128)}, f32[8,2,128,128]{3,2,1,0:T(8,128)}), (f32[8,128,128]{1,2,0:T(8,128)}, f32[8,2,128,128]{3,2,1,0:T(8,128)})) %all-reduce.22.cloned.1.call-update) | async-done | bytes 1572880 | tf_op jit(solution)/shard_map/psum | solution.py:45
  1032.7 1.2 multiply_add_fusion
  1034.1 1.1 fusion.19
  1035.2 93.8 %custom-call.20 = f32[8,128,128]{2,1,0:T(8,128)S(1)} custom-call(f32[8,128,128]{2,1,0:T(8,128)S(1)} %fusion.19), custom_call_target="Cholesky" | custom-call | tf_op jit(solution)/shard_map/jit(cholesky)/cholesky | solution.py:11
  1129.3 78.6 %custom-call.21 = f32[8,1,128,128]{2,3,1,0:T(8,128)S(1)} custom-call(f32[8,1,128,128]{3,2,1,0:T(8,128)S(1)} %select_bitcast_fusion), custom_call_target="InvertDiagBlocksLowerTriangular" | custom-call | tf_op jit(solution)/shard_map/vmap(jit(_cho_solve))/triangular_solve | solution.py:12
  1209.4 1.2 fusion.4
  (89 shorter events, 21.0 us)
Async XLA Ops:
  7.2 51.9 %all-reduce.14.cloned.1.call-start = ((), (), s32[]{:S(2)}) async-start(), calls=%async_computation | async-start | bytes 262144 | tf_op jit(solution)/shard_map/psum | solution.py:40
  21.8 114.9 %all-reduce.28.cloned.1.call-start = ((), (), s32[]{:S(2)}) async-start(), calls=%async_computation.7 | async-start | bytes 3145728 | tf_op jit(solution)/shard_map/psum | solution.py:45
  75.8 236.1 %copy-start.1 = (f32[8,128,32]{1,2,0:T(8,128)S(1)}, f32[8,128,32]{1,2,0:T(8,128)}, u32[]{:S(2)}) copy-start(f32[8,128,32]{1,2,0:T(8,128)} %all-reduce.14.cloned.1.call-done) | copy-start | bytes 393220
  78.7 273.7 %all-reduce.16.cloned.1.call-start = ((), (), s32[]{:S(2)}) async-start(), calls=%async_computation.1 | async-start | bytes 262144 | tf_op jit(solution)/shard_map/psum | solution.py:40
  136.7 176.7 %copy-start.5 = (f32[8,2,128,128]{3,2,1,0:T(8,128)S(1)}, f32[8,2,128,128]{3,2,1,0:T(8,128)}, u32[]{:S(2)}) copy-start(f32[8,2,128,128]{3,2,1,0:T(8,128)} %get-tuple-element.25) | copy-start | bytes 3145732
  318.5 111.8 %all-reduce.26.cloned.1.call-start = ((), (), s32[]{:S(2)}) async-start(), calls=%async_computation.6 | async-start | bytes 3145728 | tf_op jit(solution)/shard_map/psum | solution.py:45
  369.3 236.1 %copy-start.3 = (f32[8,128,32]{1,2,0:T(8,128)S(1)}, f32[8,128,32]{1,2,0:T(8,128)}, u32[]{:S(2)}) copy-start(f32[8,128,32]{1,2,0:T(8,128)} %all-reduce.16.cloned.1.call-done) | copy-start | bytes 393220
  372.2 273.7 %all-reduce.18.cloned.1.call-start = ((), (), s32[]{:S(2)}) async-start(), calls=%async_computation.2 | async-start | bytes 262144 | tf_op jit(solution)/shard_map/psum | solution.py:40
  430.2 176.7 %copy-start.7 = (f32[8,2,128,128]{3,2,1,0:T(8,128)S(1)}, f32[8,2,128,128]{3,2,1,0:T(8,128)}, u32[]{:S(2)}) copy-start(f32[8,2,128,128]{3,2,1,0:T(8,128)} %get-tuple-element.23) | copy-start | bytes 3145732
  612.0 112.0 %all-reduce.24.cloned.1.call-start = ((), (), s32[]{:S(2)}) async-start(), calls=%async_computation.5 | async-start | bytes 3145728 | tf_op jit(solution)/shard_map/psum | solution.py:45
  663.1 236.1 %copy-start.2 = (f32[8,128,32]{1,2,0:T(8,128)S(1)}, f32[8,128,32]{1,2,0:T(8,128)}, u32[]{:S(2)}) copy-start(f32[8,128,32]{1,2,0:T(8,128)} %all-reduce.18.cloned.1.call-done) | copy-start | bytes 393220
  666.0 273.7 %all-reduce.20.cloned.1.call-start = ((), (), s32[]{:S(2)}) async-start(), calls=%async_computation.3 | async-start | bytes 262144 | tf_op jit(solution)/shard_map/psum | solution.py:40
  724.0 176.7 %copy-start.6 = (f32[8,2,128,128]{3,2,1,0:T(8,128)S(1)}, f32[8,2,128,128]{3,2,1,0:T(8,128)}, u32[]{:S(2)}) copy-start(f32[8,2,128,128]{3,2,1,0:T(8,128)} %get-tuple-element.21) | copy-start | bytes 3145732
  905.7 127.0 %all-reduce.22.cloned.1.call-start = ((), (), s32[]{:S(2)}) async-start(), calls=%async_computation.4 | async-start | bytes 3145728 | tf_op jit(solution)/shard_map/psum | solution.py:45
  971.7 236.2 %copy-start = (f32[8,128,32]{1,2,0:T(8,128)S(1)}, f32[8,128,32]{1,2,0:T(8,128)}, u32[]{:S(2)}) copy-start(f32[8,128,32]{1,2,0:T(8,128)} %all-reduce.20.cloned.1.call-done) | copy-start | bytes 393220
  1032.7 176.7 %copy-start.4 = (f32[8,2,128,128]{3,2,1,0:T(8,128)S(1)}, f32[8,2,128,128]{3,2,1,0:T(8,128)}, u32[]{:S(2)}) copy-start(f32[8,2,128,128]{3,2,1,0:T(8,128)} %get-tuple-element.19) | copy-start | bytes 3145732
Sparse Core Ops, SparseCore 0:
  21.9 37.1 all-reduce.13
  78.8 57.8 all-reduce.27
  318.6 33.7 all-reduce.15
  372.3 57.8 all-reduce.25
  612.1 33.7 all-reduce.17
  666.1 57.8 all-reduce.23
  905.9 33.7 all-reduce.19
  974.7 57.9 all-reduce.21
where the time goes:
time: 1220 us
  other arithmetic  709 us (58%)
  waiting for transfers between devices  365 us (30%)
  blocking collectives  61.3 us (5%)
  matrix products  52.9 us (4%)
  between operations  26.4 us (2%)
    another operation x13, other arithmetic, solve_blocks(): factor = jnp.linalg.cholesky(moment)  376 us
    another operation x9, other arithmetic, solve_blocks(): jax.scipy.linalg.cho_solve((lower, True), right)  315 us
    psum x4, waiting for transfers between devices, shards(): lax.psum((jnp.einsum('bim,bjm->bij', anomaly, anomaly, precision=precise)...  227 us
    psum x4, waiting for transfers between devices, shards(): image = lax.psum(partial_value, 'st')  137 us
    psum x4, blocking collectives, shards(): center = lax.psum(jnp.sum(image, axis=2), 'mem') / members  48.9 us
  transfers between devices with their start and end apart: 8, of which 8 were waited for; matrix products, arithmetic and copies ran while one was open for 0% of the time, Pallas kernels for 0%

commit v1 on v0

--- a/solution.py
+++ b/solution.py
@@ -37,7 +37,9 @@
         picked = jnp.einsum("ps,sim->pim", selector, states, precision=precise)
         picked = picked.reshape(obs_blocks, col_count, block_size, mem_dev)
         partial_value = jnp.einsum("bkij,bkjm->bim", operator_now, picked, precision=precise)
-        image = lax.psum(partial_value, "st")
+        image = partial_value
+        for hop in (1, 2):
+            image = image + lax.ppermute(image, "st", [(dev, dev ^ hop) for dev in range(4)])
         misfit = (values_now[:, :, None] - image) / sigma_now[:, :, None]
         loglik = loglik - 0.5 * temper * jnp.sum(misfit * misfit, axis=(0, 1))
         center = lax.psum(jnp.sum(image, axis=2), "mem") / members

time: 1220 us -> 1130 us (0.926)
  waiting for transfers between devices: 365 us -> 262 us
  starting transfers between devices: 0.5 us -> 19 us
    psum x4 -> x0, waiting for transfers between devices: 137 us -> none  [shards(): image = lax.psum(partial_value, 'st')]
    ppermute x0 -> x8, waiting for transfers between devices: none -> 32 us  [shards(): lax.ppermute(image, 'st', [(dev, dev ^ hop) for dev in range(4)])]
    ppermute x0 -> x8, starting transfers between devices: none -> 18.7 us  [shards(): lax.ppermute(image, 'st', [(dev, dev ^ hop) for dev in range(4)])]
  transfers between devices with their start and end apart: 8 -> 12, of which waited for: 8 -> 12; matrix products, arithmetic and copies ran while one was open for 0% -> 0% of each run, Pallas kernels for 0% -> 0%
where the time goes in v1:
time: 1130 us; the launch traced here: 1120 us
  other arithmetic  705 us (62%)
  waiting for transfers between devices  262 us (23%)
  blocking collectives  61.4 us (5%)
  matrix products  42.4 us (4%)
  between operations  26 us (2%)
  starting transfers between devices  19 us (2%)
    another operation x13, other arithmetic, solve_blocks(): factor = jnp.linalg.cholesky(moment)  376 us
    another operation x9, other arithmetic, solve_blocks(): jax.scipy.linalg.cho_solve((lower, True), right)  315 us
    psum x4, waiting for transfers between devices, shards(): lax.psum((jnp.einsum('bim,bjm->bij', anomaly, anomaly, precision=precise)...  230 us
    psum x4, blocking collectives, shards(): center = lax.psum(jnp.sum(image, axis=2), 'mem') / members  49 us
    ppermute x8, waiting for transfers between devices, shards(): lax.ppermute(image, 'st', [(dev, dev ^ hop) for dev in range(4)])  32 us
  transfers between devices with their start and end apart: 12, of which 12 were waited for; matrix products, arithmetic and copies ran while one was open for 0% of the time, Pallas kernels for 0%

profile of v1, /device:TPU:0, one launch (start us, length us, event | category | flops | bytes accessed | tf_op | source)
XLA Modules:
  0.0 1121.6 jit_solution(15546224544905558509)
XLA Ops:
  7.2 1.5 fusion.151
  18.7 2.4 convolution_bitcast_fusion.7
  21.1 3.1 collective-permute-start
  24.2 3.5 collective-permute-done
  27.7 2.8 collective-permute-start.1
  32.0 4.2 collective-permute-done.1
  36.3 11.8 %psum.98 = f32[8,128]{1,0:T(8,128)S(1)} all-reduce(f32[8,128]{1,0:T(8,128)S(1)} %get-tuple-element.6), channel_id=1, replica_groups=mesh['mem'=8,'st'=4] {'mem'}, use_global_device_ids=true, to_apply=%region_1.2 | all-reduce | flops 1024 | bytes 8192 | tf_op jit(solution)/shard_map/psum | solution.py:45
  48.1 3.0 fusion.50
  51.1 1.8 fusion.77
  53.5 59.1 %all-reduce.16.cloned.1.call-done = (f32[8,128,128]{1,2,0:T(8,128)}, f32[8,2,128,128]{3,2,1,0:T(8,128)}) async-done(((f32[8,128,128]{1,2,0:T(8,128)}, f32[8,2,128,128]{3,2,1,0:T(8,128)}), (f32[8,128,128]{1,2,0:T(8,128)}, f32[8,2,128,128]{3,2,1,0:T(8,128)})) %all-reduce.16.cloned.1.call-update) | async-done | bytes 1572880 | tf_op jit(solution)/shard_map/psum | solution.py:47
  115.1 93.8 %custom-call.14 = f32[8,128,128]{2,1,0:T(8,128)S(1)} custom-call(f32[8,128,128]{2,1,0:T(8,128)S(1)} %fusion.31), custom_call_target="Cholesky" | custom-call | tf_op jit(solution)/shard_map/jit(cholesky)/cholesky | solution.py:11
  209.2 78.6 %custom-call.15 = f32[8,1,128,128]{2,3,1,0:T(8,128)S(1)} custom-call(f32[8,1,128,128]{3,2,1,0:T(8,128)S(1)} %select_bitcast_fusion.3), custom_call_target="InvertDiagBlocksLowerTriangular" | custom-call | tf_op jit(solution)/shard_map/vmap(jit(_cho_solve))/triangular_solve | solution.py:12
  291.2 2.4 convolution_bitcast_fusion.6
  293.7 1.7 collective-permute-start.2
  295.4 3.4 collective-permute-done.2
  298.7 2.6 collective-permute-start.3
  301.3 4.7 collective-permute-done.3
  306.2 12.0 %psum.101 = f32[8,128]{1,0:T(8,128)S(1)} all-reduce(f32[8,128]{1,0:T(8,128)S(1)} %get-tuple-element.8), channel_id=1, replica_groups=mesh['mem'=8,'st'=4] {'mem'}, use_global_device_ids=true, to_apply=%region_7.10 | all-reduce | flops 1024 | bytes 8192 | tf_op jit(solution)/shard_map/psum | solution.py:45
  318.3 3.0 fusion.47
  321.3 1.8 fusion.73
  323.3 58.2 %all-reduce.14.cloned.1.call-done = (f32[8,128,128]{1,2,0:T(8,128)}, f32[8,2,128,128]{3,2,1,0:T(8,128)}) async-done(((f32[8,128,128]{1,2,0:T(8,128)}, f32[8,2,128,128]{3,2,1,0:T(8,128)}), (f32[8,128,128]{1,2,0:T(8,128)}, f32[8,2,128,128]{3,2,1,0:T(8,128)})) %all-reduce.14.cloned.1.call-update) | async-done | bytes 1572880 | tf_op jit(solution)/shard_map/psum | solution.py:47
  384.0 93.8 %custom-call.16 = f32[8,128,128]{2,1,0:T(8,128)S(1)} custom-call(f32[8,128,128]{2,1,0:T(8,128)S(1)} %fusion.27), custom_call_target="Cholesky" | custom-call | tf_op jit(solution)/shard_map/jit(cholesky)/cholesky | solution.py:11
  478.1 78.6 %custom-call.17 = f32[8,1,128,128]{2,3,1,0:T(8,128)S(1)} custom-call(f32[8,1,128,128]{3,2,1,0:T(8,128)S(1)} %select_bitcast_fusion.2), custom_call_target="InvertDiagBlocksLowerTriangular" | custom-call | tf_op jit(solution)/shard_map/vmap(jit(_cho_solve))/triangular_solve | solution.py:12
  560.1 2.4 convolution_bitcast_fusion.5
  562.5 1.7 collective-permute-start.4
  564.2 3.4 collective-permute-done.4
  567.6 2.6 collective-permute-start.5
  570.2 4.7 collective-permute-done.5
  575.1 12.3 %psum.104 = f32[8,128]{1,0:T(8,128)S(1)} all-reduce(f32[8,128]{1,0:T(8,128)S(1)} %get-tuple-element.10), channel_id=1, replica_groups=mesh['mem'=8,'st'=4] {'mem'}, use_global_device_ids=true, to_apply=%region_11.14 | all-reduce | flops 1024 | bytes 8192 | tf_op jit(solution)/shard_map/psum | solution.py:45
  587.4 3.0 fusion.44
  590.4 1.8 fusion.69
  592.4 58.2 %all-reduce.12.cloned.1.call-done = (f32[8,128,128]{1,2,0:T(8,128)}, f32[8,2,128,128]{3,2,1,0:T(8,128)}) async-done(((f32[8,128,128]{1,2,0:T(8,128)}, f32[8,2,128,128]{3,2,1,0:T(8,128)}), (f32[8,128,128]{1,2,0:T(8,128)}, f32[8,2,128,128]{3,2,1,0:T(8,128)})) %all-reduce.12.cloned.1.call-update) | async-done | bytes 1572880 | tf_op jit(solution)/shard_map/psum | solution.py:47
  650.6 1.2 multiply_add_fusion.1
  653.1 93.8 %custom-call.18 = f32[8,128,128]{2,1,0:T(8,128)S(1)} custom-call(f32[8,128,128]{2,1,0:T(8,128)S(1)} %fusion.23), custom_call_target="Cholesky" | custom-call | tf_op jit(solution)/shard_map/jit(cholesky)/cholesky | solution.py:11
  747.2 78.6 %custom-call.19 = f32[8,1,128,128]{2,3,1,0:T(8,128)S(1)} custom-call(f32[8,1,128,128]{3,2,1,0:T(8,128)S(1)} %select_bitcast_fusion.1), custom_call_target="InvertDiagBlocksLowerTriangular" | custom-call | tf_op jit(solution)/shard_map/vmap(jit(_cho_solve))/triangular_solve | solution.py:12
  829.2 2.4 convolution_bitcast_fusion.4
  831.7 1.7 collective-permute-start.6
  833.3 3.4 collective-permute-done.6
  836.7 2.6 collective-permute-start.7
  839.3 4.7 collective-permute-done.7
  844.8 12.4 %pmax.7 = f32[]{:T(128)} all-reduce(f32[]{:T(128)} %get-tuple-element.28), channel_id=1, replica_groups=mesh['mem'=8,'st'=4] {'mem'}, use_global_device_ids=true, to_apply=%region_23.26 | all-reduce | flops 1 | bytes 8 | tf_op jit(solution)/shard_map/pmax | solution.py:62
  857.2 1.3 multiply_reduce_fusion.4
  858.5 12.9 %all-reduce = (f32[8,128]{1,0:T(8,128)S(1)}, f32[]{:T(128)}, f32[]{:T(128)}) all-reduce(f32[8,128]{1,0:T(8,128)S(1)} %get-tuple-element.12, f32[]{:T(128)} %get-tuple-element.14, f32[]{:T(128)} %get-tuple-element.13), channel_id=1, replica_groups=mesh['mem'=8,'st'=4] {'mem'}, use_global_device_ids=true, to_apply=%region_15.18 | all-reduce | flops 1026 | bytes 8208 | tf_op jit(solution)/shard_map/psum | solution.py:45
  871.4 3.0 fusion.41
  874.4 1.8 fusion.65
  880.0 54.6 %all-reduce.10.cloned.1.call-done = (f32[8,128,128]{1,2,0:T(8,128)}, f32[8,2,128,128]{3,2,1,0:T(8,128)}) async-done(((f32[8,128,128]{1,2,0:T(8,128)}, f32[8,2,128,128]{3,2,1,0:T(8,128)}), (f32[8,128,128]{1,2,0:T(8,128)}, f32[8,2,128,128]{3,2,1,0:T(8,128)})) %all-reduce.10.cloned.1.call-update) | async-done | bytes 1572880 | tf_op jit(solution)/shard_map/psum | solution.py:47
  937.1 93.8 %custom-call.20 = f32[8,128,128]{2,1,0:T(8,128)S(1)} custom-call(f32[8,128,128]{2,1,0:T(8,128)S(1)} %fusion.19), custom_call_target="Cholesky" | custom-call | tf_op jit(solution)/shard_map/jit(cholesky)/cholesky | solution.py:11
  1031.2 78.6 %custom-call.21 = f32[8,1,128,128]{2,3,1,0:T(8,128)S(1)} custom-call(f32[8,1,128,128]{3,2,1,0:T(8,128)S(1)} %select_bitcast_fusion), custom_call_target="InvertDiagBlocksLowerTriangular" | custom-call | tf_op jit(solution)/shard_map/vmap(jit(_cho_solve))/triangular_solve | solution.py:12
  (89 shorter events, 31.2 us)
Async XLA Ops:
  7.2 105.4 %all-reduce.16.cloned.1.call-start = ((), (), s32[]{:S(2)}) async-start(), calls=%async_computation.3 | async-start | bytes 3145728 | tf_op jit(solution)/shard_map/psum | solution.py:47
  21.1 6.6 collective-permute-start
  27.7 8.5 collective-permute-start.1
  52.9 328.6 %all-reduce.14.cloned.1.call-start = ((), (), s32[]{:S(2)}) async-start(), calls=%async_computation.2 | async-start | bytes 3145728 | tf_op jit(solution)/shard_map/psum | solution.py:47
  112.6 176.7 %copy-start.1 = (f32[8,2,128,128]{3,2,1,0:T(8,128)S(1)}, f32[8,2,128,128]{3,2,1,0:T(8,128)}, u32[]{:S(2)}) copy-start(f32[8,2,128,128]{3,2,1,0:T(8,128)} %get-tuple-element.25) | copy-start | bytes 3145732
  293.7 5.0 collective-permute-start.2
  298.7 7.3 collective-permute-start.3
  323.1 327.5 %all-reduce.12.cloned.1.call-start = ((), (), s32[]{:S(2)}) async-start(), calls=%async_computation.1 | async-start | bytes 3145728 | tf_op jit(solution)/shard_map/psum | solution.py:47
  381.5 176.7 %copy-start.3 = (f32[8,2,128,128]{3,2,1,0:T(8,128)S(1)}, f32[8,2,128,128]{3,2,1,0:T(8,128)}, u32[]{:S(2)}) copy-start(f32[8,2,128,128]{3,2,1,0:T(8,128)} %get-tuple-element.23) | copy-start | bytes 3145732
  562.5 5.0 collective-permute-start.4
  567.6 7.3 collective-permute-start.5
  592.2 342.4 %all-reduce.10.cloned.1.call-start = ((), (), s32[]{:S(2)}) async-start(), calls=%async_computation | async-start | bytes 3145728 | tf_op jit(solution)/shard_map/psum | solution.py:47
  650.6 176.7 %copy-start.2 = (f32[8,2,128,128]{3,2,1,0:T(8,128)S(1)}, f32[8,2,128,128]{3,2,1,0:T(8,128)}, u32[]{:S(2)}) copy-start(f32[8,2,128,128]{3,2,1,0:T(8,128)} %get-tuple-element.21) | copy-start | bytes 3145732
  831.7 5.0 collective-permute-start.6
  836.7 7.3 collective-permute-start.7
  934.6 176.7 %copy-start = (f32[8,2,128,128]{3,2,1,0:T(8,128)S(1)}, f32[8,2,128,128]{3,2,1,0:T(8,128)}, u32[]{:S(2)}) copy-start(f32[8,2,128,128]{3,2,1,0:T(8,128)} %get-tuple-element.19) | copy-start | bytes 3145732
Sparse Core Ops, SparseCore 0:
  53.0 59.5 all-reduce.15
  323.2 58.2 all-reduce.13
  592.3 58.2 all-reduce.11
  876.3 58.2 all-reduce.9
